TPU v7x, 32 devices: a whole 2x2x4 slice. The times are simulated.
32 devices in a mesh: batch: 8 (over z, y), mp: 4 (over x, core).
Axes of the slice: x: 2, y: 2, z: 4, core: 2. Of those that a mesh axis runs over, the one named last changes fastest.
Arguments:
- gate_act: bfloat16 [6144, 14336], P('batch', 'mp'), may hold values from -6 to 6
- up_act: bfloat16 [6144, 14336], P('batch', 'mp'), may hold values from -6 to 6
- upstream: bfloat16 [6144, 8192], P('batch', 'mp'), may hold values from -6 to 6
- kept_index: int32 [8, 8], P('batch'), may hold values from 0 to 31, as said below
- kept_count: int32 [8], P('batch'), may hold values from 1 to 8, as said below
Outputs:
- grad_down: bfloat16 [8192, 14336], P('batch', 'mp')
Inputs may be any that keep to these rules, and one draw needn't show every extreme that they name: `kept_index`: each group's row names different candidates; only the first kept_count entries of a row are kept. `kept_count`: the counts sum to 8 * 4 over the groups, and some group keeps exactly 8.
All inputs are finite; a program needn't handle non-finite values.
Results may differ from a plain program's by a relative error of at most 0.0049.
Values may be sent and summed in bfloat16 or wider, within the bound.
A program may use at most 128 MiB of HBM per device.

v0:
```python
import math

import jax
import jax.numpy as jnp
from jax import lax
from jax.sharding import PartitionSpec as P

SEQ = 24
CAND = 32


def on_device(gate_act, up_act, upstream, kept_index, kept_count):
    groups = lax.axis_size("batch")
    share = groups // 2
    keep_most = kept_index.shape[1]
    hidden_width = gate_act.shape[1]
    model_part = upstream.shape[1]
    gate_all = gate_act.reshape(CAND, SEQ, hidden_width)
    up_all = up_act.reshape(CAND, SEQ, hidden_width)
    grad_all = upstream.reshape(CAND, SEQ, model_part)
    picked = kept_index[0]
    counts = lax.all_gather(kept_count, "batch", axis=0, tiled=True)
    starts = jnp.cumsum(counts) - counts
    myself = lax.axis_index("batch")
    targets = jnp.arange(groups, dtype=jnp.int32)
    my_slot = jnp.mod(targets - starts[myself], groups)
    present = my_slot < counts[myself]
    seq_ids = picked[jnp.minimum(my_slot, keep_most - 1)]
    hidden = (
        jax.nn.silu(gate_all[seq_ids].astype(jnp.float32)) * up_all[seq_ids].astype(jnp.float32)
    ).astype(jnp.bfloat16)
    hidden_out = jnp.where(present[:, None, None], hidden, jnp.zeros_like(hidden))
    grad_out = grad_all[seq_ids]
    hidden_in, grad_in = (
        lax.all_to_all(hidden_out, "batch", split_axis=0, concat_axis=0, tiled=True),
        lax.all_to_all(grad_out, "batch", split_axis=0, concat_axis=0, tiled=True),
    )
    arrived = jnp.mod(myself - starts, groups) < counts
    chosen = jnp.argsort(1 - arrived.astype(jnp.int32), stable=True)[:share]
    hidden_rows = hidden_in[chosen].reshape(share * SEQ, hidden_width)
    grad_rows = grad_in[chosen].reshape(share * SEQ, model_part)
    full_width = lax.all_gather(grad_rows, "mp", axis=1, tiled=True)
    columns = lax.all_to_all(full_width, "batch", split_axis=1, concat_axis=0, tiled=True)
    summed = lax.dot_general(
        columns,
        lax.all_gather(hidden_rows, "batch", axis=0, tiled=True),
        (((0,), (0,)), ((), ())),
        preferred_element_type=jnp.float32,
    )
    factor = 1.0 / math.sqrt(groups * share * SEQ)
    return (summed * factor).astype(jnp.bfloat16)


def solution(mesh):
    placed = (P("batch", "mp"), P("batch", "mp"), P("batch", "mp"), P("batch", None), P("batch"))
    return jax.shard_map(
        on_device, mesh=mesh, in_specs=placed, out_specs=P("batch", "mp"), check_vma=False
    )
```

profile of v0, /device:TPU:1, one launch (start us, length us, event | category | flops | bytes accessed | tf_op | source)
XLA Modules:
  0.0 215.9 jit_solution(4112580387159058532)
XLA Ops:
  6.5 0.0 copy-start
  7.3 1.4 dynamic-slice
  8.7 0.8 dynamic-update-slice
  9.5 9.5 %all-reduce = s32[8]{0:T(128)S(1)} all-reduce(s32[8]{0:T(128)S(1)} %dynamic-update-slice), channel_id=1, replica_groups=mesh['batch'=8,'mp'=4] {'batch'}, use_global_device_ids=true, to_apply=%add | all-reduce | flops 8 | bytes 64
  19.0 0.2 reduce-window.9
  19.2 0.6 dynamic_slice.6
  19.8 0.6 fusion.11
  20.4 1.3 gather_fusion
  21.7 0.0 copy-done
  21.7 1.5 gather_fusion.1
  23.2 4.2 %all-to-all-start = ((bf16[8,24,2048]{2,1,0:T(8,128)(2,1)}), bf16[8,24,2048]{2,1,0:T(8,128)(2,1)}, u32[]{:S(2)}, u32[]{:S(2)}) async-start(bf16[8,24,2048]{2,1,0:T(8,128)(2,1)} %gather_fusion.1), calls=%async_computation | async-start | bytes 1572864 | tf_op jit(solution)/shard_map/all_to_all | solution.py:36
  27.4 0.6 dynamic_slice.7
  28.1 4.3 %gather_fusion.4 = bf16[8,24,3584]{2,1,0:T(8,128)(2,1)} fusion(bf16[32,24,3584]{2,1,0:T(8,128)(2,1)} %bitcast.35, s32[1024]{0:T(1024)S(1)} %pad_clamp_fusion.1), kind=kCustom, calls=%fused_computation.4 | custom fusion | bytes 2752544 | tf_op jit(solution)/shard_map/gather | solution.py:30
  32.3 4.3 %gather_fusion.3 = bf16[8,24,3584]{2,1,0:T(8,128)(2,1)} fusion(bf16[32,24,3584]{2,1,0:T(8,128)(2,1)} %bitcast.36, s32[1024]{0:T(1024)S(1)} %pad_clamp_fusion.1), kind=kCustom, calls=%fused_computation.3 | custom fusion | bytes 2752544 | tf_op jit(solution)/shard_map/gather | solution.py:30
  36.6 0.9 sort.17
  37.5 1.2 fusion.7
  38.8 3.7 %fusion.5 = bf16[8,24,3584]{2,1,0:T(8,128)(2,1)} fusion(bf16[8,24,3584]{2,1,0:T(8,128)(2,1)} %gather_fusion.4, bf16[8,24,3584]{2,1,0:T(8,128)(2,1)} %gather_fusion.3, pred[8]{0:T(512)(128)(4,1)S(1)} %fusion.7), kind=kLoop, calls=%fused_computation.15 | loop fusion | flops 6193152 | bytes 4128776 | tf_op jit(solution)/shard_map/jit(_where)/select_n | solution.py:32
  42.5 2.6 %all-to-all-done = bf16[8,24,2048]{2,1,0:T(8,128)(2,1)} async-done(((bf16[8,24,2048]{2,1,0:T(8,128)(2,1)}), bf16[8,24,2048]{2,1,0:T(8,128)(2,1)}, u32[]{:S(2)}, u32[]{:S(2)}) %all-to-all-start) | async-done | bytes 786464 | tf_op jit(solution)/shard_map/all_to_all | solution.py:36
  45.1 5.0 %all-to-all-start.2 = ((bf16[8,24,3584]{2,1,0:T(8,128)(2,1)}), bf16[8,24,3584]{2,1,0:T(8,128)(2,1)}, u32[]{:S(2)}, u32[]{:S(2)}) async-start(bf16[8,24,3584]{2,1,0:T(8,128)(2,1)} %fusion.5), calls=%async_computation.2 | async-start | bytes 2752512 | tf_op jit(solution)/shard_map/all_to_all | solution.py:35
  50.2 0.0 all-gather.3.cloned.1.call-start
  50.2 2.5 %gather_fusion.2 = bf16[4,24,2048]{2,1,0:T(8,128)(2,1)} fusion(bf16[8,24,2048]{2,1,0:T(8,128)(2,1)} %all-to-all-done, s32[1024]{0:T(1024)S(1)} %pad_clamp_fusion), kind=kCustom, calls=%fused_computation.2 | custom fusion | bytes 786448 | tf_op jit(solution)/shard_map/gather | solution.py:41
  52.7 0.0 all-gather.3.cloned.1.call-update
  52.7 0.0 all-gather.5.cloned.1.call-start
  52.8 28.0 %all-to-all-done.2 = bf16[8,24,3584]{2,1,0:T(8,128)(2,1)} async-done(((bf16[8,24,3584]{2,1,0:T(8,128)(2,1)}), bf16[8,24,3584]{2,1,0:T(8,128)(2,1)}, u32[]{:S(2)}, u32[]{:S(2)}) %all-to-all-start.2) | async-done | bytes 1376288 | tf_op jit(solution)/shard_map/all_to_all | solution.py:35
  80.8 2.8 %gather_fusion.5 = bf16[4,24,3584]{2,1,0:T(8,128)(2,1)} fusion(bf16[8,24,3584]{2,1,0:T(8,128)(2,1)} %all-to-all-done.2, s32[1024]{0:T(1024)S(1)} %pad_clamp_fusion), kind=kCustom, calls=%fused_computation.5 | custom fusion | bytes 1376272 | tf_op jit(solution)/shard_map/gather | solution.py:40
  83.5 0.0 all-gather.5.cloned.1.call-update
  83.6 0.0 all-gather.3.cloned.1.call-done
  83.6 1.5 copy.10
  85.2 64.1 %all_to_all.29 = bf16[96,8,1024]{2,0,1:T(8,128)(2,1)} all-to-all(bf16[96,8,1024]{2,0,1:T(8,128)(2,1)S(1)} %bitcast.30), channel_id=1, replica_groups=mesh['batch'=8,'mp'=4] {'batch'}, dimensions={1} | all-to-all | bytes 3145728 | tf_op jit(solution)/shard_map/all_to_all | solution.py:43
  149.3 49.5 %all-gather.5.cloned.1.call-done = bf16[768,3584]{1,0:T(8,128)(2,1)} async-done(((bf16[96,3584]{1,0:T(8,128)(2,1)}), bf16[768,3584]{1,0:T(8,128)(2,1)}) %all-gather.5.cloned.1.call-update) | async-done | bytes 5505040 | tf_op jit(solution)/shard_map/all_gather | solution.py:46
  198.8 10.3 %multiply_convert_fusion = bf16[1024,3584]{1,0:T(8,128)(2,1)} fusion(bf16[768,1024]{1,0:T(8,128)(2,1)} %bitcast.33, bf16[768,3584]{1,0:T(8,128)(2,1)} %all-gather.5.cloned.1.call-done), kind=kOutput, calls=%fused_computation.6 | convolution fusion | flops 5644484608 | bytes 14417920 | tf_op jit(solution)/shard_map/dot_general | solution.py:44
  (8 shorter events, 0.1 us)
Async XLA Ops:
  6.5 15.2 %copy-start = (bf16[768,2048]{1,0:T(8,128)(2,1)S(1)}, bf16[768,2048]{1,0:T(8,128)(2,1)}, u32[]{:S(2)}) copy-start(bf16[768,2048]{1,0:T(8,128)(2,1)} %param.7) | copy-start | bytes 9437188
  23.2 21.9 %all-to-all-start = ((bf16[8,24,2048]{2,1,0:T(8,128)(2,1)}), bf16[8,24,2048]{2,1,0:T(8,128)(2,1)}, u32[]{:S(2)}, u32[]{:S(2)}) async-start(bf16[8,24,2048]{2,1,0:T(8,128)(2,1)} %gather_fusion.1), calls=%async_computation | async-start | bytes 1572864 | tf_op jit(solution)/shard_map/all_to_all | solution.py:36
  45.1 35.6 %all-to-all-start.2 = ((bf16[8,24,3584]{2,1,0:T(8,128)(2,1)}), bf16[8,24,3584]{2,1,0:T(8,128)(2,1)}, u32[]{:S(2)}, u32[]{:S(2)}) async-start(bf16[8,24,3584]{2,1,0:T(8,128)(2,1)} %fusion.5), calls=%async_computation.2 | async-start | bytes 2752512 | tf_op jit(solution)/shard_map/all_to_all | solution.py:35
  50.2 33.4 %all-gather.3.cloned.1.call-start = ((), (), s32[]{:S(2)}) async-start(), calls=%async_computation.3 | async-start | bytes 1966080 | tf_op jit(solution)/shard_map/all_gather | solution.py:42
  52.7 146.1 %all-gather.5.cloned.1.call-start = ((), (), s32[]{:S(2)}) async-start(), calls=%async_computation.4 | async-start | bytes 6193152 | tf_op jit(solution)/shard_map/all_gather | solution.py:46
Sparse Core Ops, SparseCore 0:
  52.8 23.3 all-gather.2
  83.7 115.0 all-gather.4
where the time goes:
time: 219 us; the launch traced here: 216 us
  waiting for transfers between devices  80.2 us (37%)
  blocking collectives  73.7 us (34%)
  local copies, waits for them, and re-layouts  21.5 us (10%)
  between operations  14.3 us (7%)
  matrix products  10.3 us (5%)
  starting transfers between devices  9.33 us (4%)
  other arithmetic  6.7 us (3%)
    all_to_all x1, blocking collectives, on_device(): lax.all_to_all(full_width, 'batch', split_axis=1, concat_axis=0, tiled=True)  64.1 us
    all_gather x1, waiting for transfers between devices, on_device(): lax.all_gather(hidden_rows, 'batch', axis=0, tiled=True)  49.5 us
    all_to_all x1, waiting for transfers between devices, on_device(): lax.all_to_all(hidden_out, 'batch', split_axis=0, concat_axis=0, tiled=True)  28 us
    dot_general x1, matrix products, on_device(): lax.dot_general(columns, lax.all_gather(hidden_rows, 'batch', axis=0, til...  10.3 us
    unnamed x1, blocking collectives  9.54 us
    all_to_all x1, starting transfers between devices, on_device(): lax.all_to_all(hidden_out, 'batch', split_axis=0, concat_axis=0, tiled=True)  5.04 us
  transfers between devices with their start and end apart: 4, of which 3 were waited for; matrix products, arithmetic and copies ran while one was open for 10% of the time, Pallas kernels for 0%

commit v1 on v0

v1 whole, which is shorter than its diff:
```python
import functools
import math

import jax
import jax.numpy as jnp
from jax import lax
from jax.experimental import pallas as pl
from jax.experimental.pallas import tpu as pltpu
from jax.sharding import PartitionSpec as P

SEQ = 24
CAND = 32
MESH = pl.DeviceIdType.MESH
LEAD = 2


def pick_kernel(index_ref, gate_ref, up_ref, up_grad_ref, hidden_ref, grad_ref):
    gate = gate_ref[...].astype(jnp.float32)
    hidden_ref[...] = (jax.nn.silu(gate) * up_ref[...].astype(jnp.float32)).astype(jnp.bfloat16)
    grad_ref[...] = up_grad_ref[...]


def pick(picked, gate_all, up_all, grad_all):
    keep_most = picked.shape[0]

    def block(width):
        return pl.BlockSpec((1, SEQ, width), lambda j, index: (index[j], 0, 0))

    def out_block(width):
        return pl.BlockSpec((1, SEQ, width), lambda j, index: (j, 0, 0))

    wide, part = gate_all.shape[2], grad_all.shape[2]
    return pl.pallas_call(
        pick_kernel,
        grid_spec=pltpu.PrefetchScalarGridSpec(
            num_scalar_prefetch=1,
            grid=(keep_most,),
            in_specs=[block(wide), block(wide), block(part)],
            out_specs=[out_block(wide), out_block(part)],
        ),
        out_shape=[
            jax.ShapeDtypeStruct((keep_most, SEQ, wide), jnp.bfloat16),
            jax.ShapeDtypeStruct((keep_most, SEQ, part), jnp.bfloat16),
        ],
    )(picked, gate_all, up_all, grad_all)


def exchange_kernel(
    groups, parts, keep_most, total,
    starts_ref, hid_ref, grad_ref, out_ref, gout_ref,
    y_send, y_recv, loc, dn_recv, dn_send, up_recv, up_send, ga, gb, gc,
    ys_sem, yr_sem, dns_sem, dnr_sem, ups_sem, upr_sem, fs_sem, fr_sem,
    as_sem, ar_sem, bs_sem, br_sem, cs_sem, cr_sem, l_sem,
):
    b, m = lax.axis_index("batch"), lax.axis_index("mp")
    planes, pairs = groups // 2, total // 2
    z, y = b // 2, lax.rem(b, 2)
    peer = z * 2 + 1 - y
    ks = keep_most // parts
    ratio = groups // parts
    block = grad_ref.shape[2] // ratio

    def low(plane):
        return jnp.maximum(2 * plane, total - 2 * keep_most * (planes - plane)) // 2

    def high(plane):
        return (jnp.minimum(2 * keep_most * plane, total - 2 * (planes - plane)) + 1) // 2

    barrier = pltpu.get_barrier_semaphore()
    for d in range(1, groups):
        pl.semaphore_signal(barrier, inc=1, device_id=(lax.rem(b + d, groups), m), device_id_type=MESH)
    for d in range(1, parts):
        pl.semaphore_signal(barrier, inc=1, device_id=(b, lax.rem(m + d, parts)), device_id_type=MESH)
    pl.semaphore_wait(barrier, groups + parts - 2)

    def copy_a(d):
        other = lax.rem(m + d, parts)
        return pltpu.make_async_remote_copy(
            src_ref=grad_ref.at[pl.ds(other * ks, ks)], dst_ref=ga.at[m],
            send_sem=as_sem.at[d], recv_sem=ar_sem.at[d],
            device_id=(b, other), device_id_type=MESH)

    def copy_b(d):
        other = lax.rem(b + d, groups)
        return pltpu.make_async_remote_copy(
            src_ref=ga.at[other // ratio, :, :, pl.ds(pl.multiple_of(lax.rem(other, ratio) * block, block), block)],
            dst_ref=gb.at[b],
            send_sem=bs_sem.at[d], recv_sem=br_sem.at[d],
            device_id=(other, m), device_id_type=MESH)

    def copy_c(d):
        other = lax.rem(m + d, parts)
        return pltpu.make_async_remote_copy(
            src_ref=gb, dst_ref=gc.at[m],
            send_sem=cs_sem.at[d], recv_sem=cr_sem.at[d],
            device_id=(b, other), device_id_type=MESH)

    def copy_y(k):
        return pltpu.make_async_remote_copy(
            src_ref=y_send.at[k], dst_ref=y_recv.at[k],
            send_sem=ys_sem.at[k], recv_sem=yr_sem.at[k],
            device_id=(peer, m), device_id_type=MESH)

    def copy_dn(p):
        return pltpu.make_async_remote_copy(
            src_ref=dn_send.at[p], dst_ref=dn_recv.at[p],
            send_sem=dns_sem.at[p], recv_sem=dnr_sem.at[p],
            device_id=(lax.rem(b + groups - 2, groups), m), device_id_type=MESH)

    def copy_up(p):
        return pltpu.make_async_remote_copy(
            src_ref=up_send.at[p], dst_ref=up_recv.at[p],
            send_sem=ups_sem.at[p], recv_sem=upr_sem.at[p],
            device_id=(lax.rem(b + 2, groups), m), device_id_type=MESH)

    def copy_f(p):
        return pltpu.make_async_remote_copy(
            src_ref=out_ref.at[p, y], dst_ref=out_ref.at[p, y],
            send_sem=fs_sem.at[p], recv_sem=fr_sem.at[p],
            device_id=(peer, m), device_id_type=MESH)

    for d in range(1, parts):
        copy_a(d).start()

    my_start, peer_start = starts_ref[b], starts_ref[peer]
    offset = lax.rem(1 - y + my_start, 2)

    @pl.loop(0, keep_most // 2)
    def _(k):
        y_send[k] = hid_ref[2 * k + offset]
        copy_y(k).start()

    own = pltpu.make_async_copy(grad_ref.at[pl.ds(m * ks, ks)], ga.at[m], l_sem.at[0])
    own.start()
    own.wait()
    for d in range(1, parts):
        copy_a(d).wait()
    for d in range(1, groups):
        copy_b(d).start()
    own = pltpu.make_async_copy(
        ga.at[b // ratio, :, :, pl.ds(pl.multiple_of(lax.rem(b, ratio) * block, block), block)], gb.at[b], l_sem.at[1])
    own.start()
    own.wait()

    @pl.loop(0, keep_most // 2)
    def _(k):
        copy_y(k).wait()

    plane_start = starts_ref[2 * z]
    plane_end = starts_ref[2 * z + 2]
    my_end = starts_ref[b + 1]

    @pl.loop(0, pairs)
    def _(p):
        number = 2 * p + y
        mine = hid_ref[jnp.clip(number - my_start, 0, keep_most - 1)]
        theirs = y_recv[jnp.clip((number - peer_start) // 2, 0, keep_most // 2 - 1)]
        is_mine = jnp.logical_and(number >= my_start, number < my_end)
        loc[p] = jnp.where(is_mine, mine, theirs)

    def gets_dn(p):
        return jnp.logical_and(z < planes - 1, p >= low(z + 1))

    def gets_up(p):
        return jnp.logical_and(z > 0, p < high(z))

    @pl.loop(0, pairs + LEAD * planes)
    def _(t):
        pd = t - LEAD * (planes - 1 - z)
        pu = t - LEAD * z
        pf = t - LEAD * planes

        @pl.when(jnp.logical_and(pd >= 0, pd < pairs))
        def _():
            @pl.when(gets_dn(pd))
            def _():
                copy_dn(pd).wait_recv()

                @pl.when(z > 0)
                def _():
                    dn_send[pd] = jnp.where(2 * pd + y >= plane_end, dn_recv[pd], loc[pd])
                    copy_dn(pd).start()

            @pl.when(jnp.logical_and(jnp.logical_not(gets_dn(pd)), jnp.logical_and(z > 0, pd >= low(z))))
            def _():
                dn_send[pd] = loc[pd]
                copy_dn(pd).start()

        @pl.when(jnp.logical_and(pu >= 0, pu < pairs))
        def _():
            @pl.when(gets_up(pu))
            def _():
                copy_up(pu).wait_recv()

                @pl.when(z < planes - 1)
                def _():
                    up_send[pu] = jnp.where(2 * pu + y < plane_start, up_recv[pu], loc[pu])
                    copy_up(pu).start()

            @pl.when(jnp.logical_and(jnp.logical_not(gets_up(pu)), jnp.logical_and(z < planes - 1, pu < high(z + 1))))
            def _():
                up_send[pu] = loc[pu]
                copy_up(pu).start()

        @pl.when(pf >= 0)
        def _():
            number = 2 * pf + y
            out_ref[pf, y] = loc[pf]

            @pl.when(gets_dn(pf))
            def _():
                out_ref[pf, y] = jnp.where(number >= plane_end, dn_recv[pf], out_ref[pf, y])

            @pl.when(gets_up(pf))
            def _():
                out_ref[pf, y] = jnp.where(number < plane_start, up_recv[pf], out_ref[pf, y])

            copy_f(pf).start()

    for d in range(1, groups):
        copy_b(d).wait()
    for d in range(1, parts):
        copy_c(d).start()
    own = pltpu.make_async_copy(gb, gc.at[m], l_sem.at[2])
    own.start()
    own.wait()
    for d in range(1, parts):
        copy_c(d).wait()

    @pl.loop(0, total)
    def _(i):
        g = jnp.int32(0)
        for q in range(1, groups):
            g = g + (starts_ref[q] <= i).astype(jnp.int32)
        j = jnp.clip(i - starts_ref[g], 0, keep_most - 1)
        gout_ref[i] = gc[j // ks, g, lax.rem(j, ks)]

    @pl.loop(0, pairs)
    def _(p):
        copy_f(p).wait_send()
        pltpu.make_async_remote_copy(
            src_ref=out_ref.at[p, 1 - y], dst_ref=out_ref.at[p, 1 - y],
            send_sem=fs_sem.at[p], recv_sem=fr_sem.at[p],
            device_id=(peer, m), device_id_type=MESH).wait_recv()

        @pl.when(jnp.logical_and(z > 0, p >= low(z)))
        def _():
            copy_dn(p).wait_send()

        @pl.when(jnp.logical_and(z < planes - 1, p < high(z + 1)))
        def _():
            copy_up(p).wait_send()


def exchange(starts, hid, grad, groups, parts, total):
    keep_most, _, wide = hid.shape
    part = grad.shape[2]
    pairs = total // 2
    ks = keep_most // parts
    block = part * parts // groups
    bf16 = jnp.bfloat16
    dma = pltpu.SemaphoreType.DMA
    chain = pltpu.VMEM((pairs, SEQ, wide), bf16)
    return pl.pallas_call(
        functools.partial(exchange_kernel, groups, parts, keep_most, total),
        out_shape=[
            jax.ShapeDtypeStruct((pairs, 2, SEQ, wide), bf16),
            jax.ShapeDtypeStruct((total, SEQ, block), bf16),
        ],
        in_specs=[
            pl.BlockSpec(memory_space=pltpu.SMEM),
            pl.BlockSpec(memory_space=pltpu.VMEM),
            pl.BlockSpec(memory_space=pltpu.VMEM),
        ],
        out_specs=[pl.BlockSpec(memory_space=pltpu.VMEM)] * 2,
        scratch_shapes=[
            pltpu.VMEM((keep_most // 2, SEQ, wide), bf16),
            pltpu.VMEM((keep_most // 2, SEQ, wide), bf16),
            chain, chain, chain, chain, chain,
            pltpu.VMEM((parts, ks, SEQ, part), bf16),
            pltpu.VMEM((groups, ks, SEQ, block), bf16),
            pltpu.VMEM((parts, groups, ks, SEQ, block), bf16),
            dma((keep_most // 2,)), dma((keep_most // 2,)),
            dma((pairs,)), dma((pairs,)), dma((pairs,)), dma((pairs,)), dma((pairs,)), dma((pairs,)),
            dma((parts,)), dma((parts,)), dma((groups,)), dma((groups,)), dma((parts,)), dma((parts,)),
            dma((3,)),
        ],
        compiler_params=pltpu.CompilerParams(
            collective_id=0, has_side_effects=True, vmem_limit_bytes=60 * 1024 * 1024
        ),
    )(starts, hid, grad)


def on_device(gate_act, up_act, upstream, kept_index, kept_count):
    groups, parts = lax.axis_size("batch"), lax.axis_size("mp")
    share = groups // 2
    total = groups * share
    wide, part = gate_act.shape[1], upstream.shape[1]
    hid, grad = pick(
        kept_index[0],
        gate_act.reshape(CAND, SEQ, wide),
        up_act.reshape(CAND, SEQ, wide),
        upstream.reshape(CAND, SEQ, part),
    )
    counts = lax.all_gather(kept_count, "batch", axis=0, tiled=True)
    starts = jnp.concatenate([jnp.zeros((1,), jnp.int32), jnp.cumsum(counts)])
    rows, columns = exchange(starts, hid, grad, groups, parts, total)
    summed = lax.dot_general(
        columns.reshape(total * SEQ, columns.shape[2]),
        rows.reshape(total * SEQ, wide),
        (((0,), (0,)), ((), ())),
        preferred_element_type=jnp.float32,
    )
    return (summed * (1.0 / math.sqrt(total * SEQ))).astype(jnp.bfloat16)


def solution(mesh):
    placed = (P("batch", "mp"), P("batch", "mp"), P("batch", "mp"), P("batch", None), P("batch"))
    return jax.shard_map(
        on_device, mesh=mesh, in_specs=placed, out_specs=P("batch", "mp"), check_vma=False
    )
```

time: 219 us -> 169 us (0.77); the launches traced: 216 us -> 169 us
  Pallas kernels: 0 us -> 146 us
  waiting for transfers between devices: 80.2 us -> 0 us
  blocking collectives: 73.7 us -> 9.54 us
  local copies, waits for them, and re-layouts: 21.5 us -> 2 us
  between operations: 14.3 us -> 0.66 us
  starting transfers between devices: 9.33 us -> 0 us
  other arithmetic: 6.7 us -> 0.83 us
    pallas_call x0 -> x2, Pallas kernels: none -> 146 us  [the longest x1 139 us: exchange(): pl.pallas_call(functools.partial(exchange_kernel, groups, parts, keep_mos...]
    all_to_all x1 -> x0, blocking collectives: 64.1 us -> none  [on_device(): lax.all_to_all(full_width, 'batch', split_axis=1, concat_axis=0, tiled=True)]
    all_gather x2 -> x0, waiting for transfers between devices: 49.5 us -> none  [the longest x1 49.5 us: on_device(): lax.all_gather(hidden_rows, 'batch', axis=0, tiled=True)]
    all_to_all x2 -> x0, waiting for transfers between devices: 30.6 us -> none  [the longest x1 28 us: on_device(): lax.all_to_all(hidden_out, 'batch', split_axis=0, concat_axis=0, tiled=True)]
    gather x6 -> x0, local copies, waits for them, and re-layouts: 16.6 us -> none  [the longest x1 4.27 us: on_device(): gate_all[seq_ids].astype(jnp.float32)]
    all_to_all x2 -> x0, starting transfers between devices: 9.25 us -> none  [the longest x1 5.04 us: on_device(): lax.all_to_all(hidden_out, 'batch', split_axis=0, concat_axis=0, tiled=True)]
    select_n x4 -> x0, other arithmetic: 4.34 us -> none  [the longest x1 3.75 us: on_device(): jnp.where(present[:, None, None], hidden, jnp.zeros_like(hidden))]
  transfers between devices with their start and end apart: 4 -> 0, of which waited for: 3 -> 0; matrix products, arithmetic and copies ran while one was open for 10% -> 0% of each run, Pallas kernels for 0% -> 0%
where the time goes in v1:
time: 169 us
  Pallas kernels  146 us (86%)
  matrix products  10.3 us (6%)
  blocking collectives  9.54 us (6%)
  local copies, waits for them, and re-layouts  2 us (1%)
    pallas_call x1, Pallas kernels, exchange(): pl.pallas_call(functools.partial(exchange_kernel, groups, parts, keep_mos...  139 us
    dot_general x1, matrix products, on_device(): lax.dot_general(columns.reshape(total * SEQ, columns.shape[2]), rows.resh...  10.3 us
    unnamed x1, blocking collectives  9.54 us
    pallas_call x1, Pallas kernels, pick(): pl.pallas_call(pick_kernel, grid_spec=pltpu.PrefetchScalarGridSpec(num_sc...  6.88 us

profile of v1, /device:TPU:1, one launch (start us, length us, event | category | flops | bytes accessed | tf_op | source)
XLA Modules:
  0.0 169.0 jit_solution(4127076749834686838)
XLA Ops:
  0.7 1.2 dynamic-slice
  1.9 0.8 dynamic-update-slice
  2.7 9.5 %all-reduce = s32[8]{0:T(128)S(1)} all-reduce(s32[8]{0:T(128)S(1)} %dynamic-update-slice), channel_id=1, replica_groups=mesh['batch'=8,'mp'=4] {'batch'}, use_global_device_ids=true, to_apply=%add | all-reduce | flops 8 | bytes 64
  12.2 0.2 reduce-window.9
  12.4 0.6 pad_add_fusion.starts_ref
  13.0 6.9 %shard_map.55 = (bf16[8,24,3584]{2,1,0:T(8,128)(2,1)}, bf16[8,24,2048]{2,1,0:T(8,128)(2,1)}) custom-call(s32[8]{0:T(128)} %bitcast.14, bf16[32,24,3584]{2,1,0:T(8,128)(2,1)} %bitcast.11, bf16[32,24,3584]{2,1,0:T(8,128)(2,1)} %bitcast.12, bf16[32,24,2048]{2,1,0:T(8,128)(2,1)} %bitcast.13), custom_call_target="tpu_custom_call" | custom-call | tf_op jit(solution)/shard_map/pallas_call | solution.py:33
  19.9 138.9 %shard_map.56 = (bf16[16,2,24,3584]{3,2,1,0:T(8,128)(2,1)}, bf16[32,24,1024]{2,1,0:T(8,128)(2,1)}) custom-call(s32[9]{0:T(128)} %pad_add_fusion.starts_ref, bf16[8,24,3584]{2,1,0:T(8,128)(2,1)} %get-tuple-element.9.hid_ref, bf16[8,24,2048]{2,1,0:T(8,128)(2,1)} %get-tuple-element.10.grad_ref), custom_call_target="tpu_custom_call" | custom-call | tf_op jit(solution)/shard_map/pallas_call | solution.py:264
  158.8 10.3 %multiply_convert_fusion = bf16[1024,3584]{1,0:T(8,128)(2,1)} fusion(bf16[768,1024]{1,0:T(8,128)(2,1)} %bitcast.16, bf16[768,3584]{1,0:T(8,128)(2,1)} %bitcast.15), kind=kOutput, calls=%fused_computation | convolution fusion | flops 5644484608 | bytes 14417920 | tf_op jit(solution)/shard_map/dot_general | solution.py:308
  (1 shorter events, 0.0 us)

commit v2 on v1

v2 whole, which is shorter than its diff:
```python
import functools
import math

import jax
import jax.numpy as jnp
from jax import lax
from jax.experimental import pallas as pl
from jax.experimental.pallas import tpu as pltpu
from jax.sharding import PartitionSpec as P

SEQ = 24
CAND = 32
MESH = pl.DeviceIdType.MESH
LEAD = 3


def pick_kernel(index_ref, gate_ref, up_ref, up_grad_ref, hidden_ref, grad_ref):
    gate = gate_ref[...].astype(jnp.float32)
    hidden_ref[...] = (jax.nn.silu(gate) * up_ref[...].astype(jnp.float32)).astype(jnp.bfloat16)
    grad_ref[...] = up_grad_ref[...]


def pick(picked, gate_all, up_all, grad_all):
    keep_most = picked.shape[0]

    def block(width):
        return pl.BlockSpec((1, SEQ, width), lambda j, index: (index[j], 0, 0))

    def out_block(width):
        return pl.BlockSpec((1, SEQ, width), lambda j, index: (j, 0, 0))

    wide, part = gate_all.shape[2], grad_all.shape[2]
    return pl.pallas_call(
        pick_kernel,
        grid_spec=pltpu.PrefetchScalarGridSpec(
            num_scalar_prefetch=1,
            grid=(keep_most,),
            in_specs=[block(wide), block(wide), block(part)],
            out_specs=[out_block(wide), out_block(part)],
        ),
        out_shape=[
            jax.ShapeDtypeStruct((keep_most, SEQ, wide), jnp.bfloat16),
            jax.ShapeDtypeStruct((keep_most, SEQ, part), jnp.bfloat16),
        ],
    )(picked, gate_all, up_all, grad_all)


def exchange_kernel(
    groups, parts, keep_most, total, chunks,
    count_ref, hid_ref, grad_ref, out_ref, gout_ref,
    counts_in, counts_ref, starts_ref,
    y_send, y_recv, loc, dn_recv, dn_send, up_recv, up_send, ga, gb, gc,
    ys_sem, yr_sem, dns_sem, dnr_sem, ups_sem, upr_sem, fs_sem, fr_sem,
    as_sem, ar_sem, bs_sem, br_sem, cs_sem, cr_sem, ns_sem, nr_sem, l_sem,
):
    b, m = lax.axis_index("batch"), lax.axis_index("mp")
    planes, pairs = groups // 2, total // 2
    z, y = b // 2, lax.rem(b, 2)
    peer = z * 2 + 1 - y
    ks = keep_most // parts
    ratio = groups // parts
    block = grad_ref.shape[2] // ratio
    width = hid_ref.shape[2] // chunks
    half = keep_most // 2
    steps = chunks * pairs

    def cols(c):
        if isinstance(c, int):
            return pl.ds(c * width, width)
        return pl.ds(pl.multiple_of(c * width, width), width)

    def low(plane):
        return jnp.maximum(2 * plane, total - 2 * keep_most * (planes - plane)) // 2

    def high(plane):
        return (jnp.minimum(2 * keep_most * plane, total - 2 * (planes - plane)) + 1) // 2

    barrier = pltpu.get_barrier_semaphore()
    for d in range(1, groups):
        pl.semaphore_signal(barrier, inc=1, device_id=(lax.rem(b + d, groups), m), device_id_type=MESH)
    for d in range(1, parts):
        pl.semaphore_signal(barrier, inc=1, device_id=(b, lax.rem(m + d, parts)), device_id_type=MESH)
    pl.semaphore_wait(barrier, groups + parts - 2)

    def copy_a(d):
        other = lax.rem(m + d, parts)
        return pltpu.make_async_remote_copy(
            src_ref=grad_ref.at[pl.ds(other * ks, ks)], dst_ref=ga.at[m],
            send_sem=as_sem.at[d], recv_sem=ar_sem.at[d],
            device_id=(b, other), device_id_type=MESH)

    def copy_b(d):
        other = lax.rem(b + d, groups)
        return pltpu.make_async_remote_copy(
            src_ref=ga.at[other // ratio, :, :, pl.ds(pl.multiple_of(lax.rem(other, ratio) * block, block), block)],
            dst_ref=gb.at[b],
            send_sem=bs_sem.at[d], recv_sem=br_sem.at[d],
            device_id=(other, m), device_id_type=MESH)

    def copy_c(d):
        other = lax.rem(m + d, parts)
        return pltpu.make_async_remote_copy(
            src_ref=gb, dst_ref=gc.at[m],
            send_sem=cs_sem.at[d], recv_sem=cr_sem.at[d],
            device_id=(b, other), device_id_type=MESH)

    def copy_n(d):
        return pltpu.make_async_remote_copy(
            src_ref=count_ref, dst_ref=counts_in.at[b],
            send_sem=ns_sem.at[d], recv_sem=nr_sem.at[d],
            device_id=(lax.rem(b + d, groups), m), device_id_type=MESH)

    def copy_y(c, k):
        return pltpu.make_async_remote_copy(
            src_ref=y_send.at[k, :, cols(c)], dst_ref=y_recv[c].at[k],
            send_sem=ys_sem.at[c * half + k], recv_sem=yr_sem.at[c * half + k],
            device_id=(peer, m), device_id_type=MESH)

    def copy_dn(s):
        p, c = lax.rem(s, pairs), s // pairs
        return pltpu.make_async_remote_copy(
            src_ref=dn_send.at[p, :, cols(c)], dst_ref=dn_recv.at[p, :, cols(c)],
            send_sem=dns_sem.at[s], recv_sem=dnr_sem.at[s],
            device_id=(lax.rem(b + groups - 2, groups), m), device_id_type=MESH)

    def copy_up(s):
        p, c = lax.rem(s, pairs), s // pairs
        return pltpu.make_async_remote_copy(
            src_ref=up_send.at[p, :, cols(c)], dst_ref=up_recv.at[p, :, cols(c)],
            send_sem=ups_sem.at[s], recv_sem=upr_sem.at[s],
            device_id=(lax.rem(b + 2, groups), m), device_id_type=MESH)

    def copy_f(s, side):
        p, c = lax.rem(s, pairs), s // pairs
        return pltpu.make_async_remote_copy(
            src_ref=out_ref.at[p, side, :, cols(c)], dst_ref=out_ref.at[p, side, :, cols(c)],
            send_sem=fs_sem.at[s], recv_sem=fr_sem.at[s],
            device_id=(peer, m), device_id_type=MESH)

    for d in range(1, groups):
        copy_n(d).start()
    own = pltpu.make_async_copy(count_ref, counts_in.at[b], l_sem.at[3])
    own.start()
    for d in range(1, parts):
        copy_a(d).start()

    own.wait()
    for d in range(1, groups):
        copy_n(d).wait()
    to_scalars = pltpu.make_async_copy(counts_in, counts_ref, l_sem.at[4])
    to_scalars.start()
    to_scalars.wait()
    before = jnp.int32(0)
    for g in range(groups):
        starts_ref[g] = before
        before = before + counts_ref[g, 0, 0]
    starts_ref[groups] = before

    my_start, peer_start = starts_ref[b], starts_ref[peer]
    offset = lax.rem(1 - y + my_start, 2)

    @pl.loop(0, half)
    def _(k):
        y_send[k] = hid_ref[2 * k + offset]
        copy_y(0, k).start()

    for c in range(1, chunks):

        @pl.loop(0, half)
        def _(k):
            copy_y(c, k).start()

    own = pltpu.make_async_copy(grad_ref.at[pl.ds(m * ks, ks)], ga.at[m], l_sem.at[0])
    own.start()
    own.wait()
    for d in range(1, parts):
        copy_a(d).wait()
    for d in range(1, groups):
        copy_b(d).start()
    own = pltpu.make_async_copy(
        ga.at[b // ratio, :, :, pl.ds(pl.multiple_of(lax.rem(b, ratio) * block, block), block)], gb.at[b], l_sem.at[1])
    own.start()
    own.wait()

    plane_start = starts_ref[2 * z]
    plane_end = starts_ref[2 * z + 2]
    my_end = starts_ref[b + 1]
    far = jnp.maximum(z, planes - 1 - z)

    def place(s, c):
        p = lax.rem(s, pairs)
        number = 2 * p + y
        mine = hid_ref[jnp.clip(number - my_start, 0, keep_most - 1), :, cols(c)]
        theirs = y_recv[c][jnp.clip((number - peer_start) // 2, 0, half - 1)]
        is_mine = jnp.logical_and(number >= my_start, number < my_end)
        loc[p, :, cols(c)] = jnp.where(is_mine, mine, theirs)

    def gets_dn(s):
        return jnp.logical_and(z < planes - 1, lax.rem(s, pairs) >= low(z + 1))

    def gets_up(s):
        return jnp.logical_and(z > 0, lax.rem(s, pairs) < high(z))

    def gives_dn(s):
        return jnp.logical_and(z > 0, lax.rem(s, pairs) >= low(z))

    def gives_up(s):
        return jnp.logical_and(z < planes - 1, lax.rem(s, pairs) < high(z + 1))

    @pl.loop(0, steps + LEAD * (planes - 1))
    def _(t):
        sd = t - LEAD * (planes - 1 - z)
        su = t - LEAD * z
        sf = t - LEAD * far

        for c in range(chunks):

            @pl.when(t == c * pairs)
            def _():
                @pl.loop(0, half)
                def _(k):
                    copy_y(c, k).wait()

            @pl.when(jnp.logical_and(t >= c * pairs, t < (c + 1) * pairs))
            def _():
                place(t, c)

        @pl.when(t == steps // 3)
        def _():
            for d in range(1, groups):
                copy_b(d).wait()
            for d in range(1, parts):
                copy_c(d).start()

        @pl.when(jnp.logical_and(sd >= 0, sd < steps))
        def _():
            p, c = lax.rem(sd, pairs), sd // pairs

            @pl.when(gets_dn(sd))
            def _():
                copy_dn(sd).wait_recv()

                @pl.when(z > 0)
                def _():
                    dn_send[p, :, cols(c)] = jnp.where(
                        2 * p + y >= plane_end, dn_recv[p, :, cols(c)], loc[p, :, cols(c)])
                    copy_dn(sd).start()

            @pl.when(jnp.logical_and(jnp.logical_not(gets_dn(sd)), gives_dn(sd)))
            def _():
                dn_send[p, :, cols(c)] = loc[p, :, cols(c)]
                copy_dn(sd).start()

        @pl.when(jnp.logical_and(su >= 0, su < steps))
        def _():
            p, c = lax.rem(su, pairs), su // pairs

            @pl.when(gets_up(su))
            def _():
                copy_up(su).wait_recv()

                @pl.when(z < planes - 1)
                def _():
                    up_send[p, :, cols(c)] = jnp.where(
                        2 * p + y < plane_start, up_recv[p, :, cols(c)], loc[p, :, cols(c)])
                    copy_up(su).start()

            @pl.when(jnp.logical_and(jnp.logical_not(gets_up(su)), gives_up(su)))
            def _():
                up_send[p, :, cols(c)] = loc[p, :, cols(c)]
                copy_up(su).start()

        @pl.when(jnp.logical_and(sf >= 0, sf < steps))
        def _():
            p, c = lax.rem(sf, pairs), sf // pairs
            number = 2 * p + y
            out_ref[p, y, :, cols(c)] = loc[p, :, cols(c)]

            @pl.when(gets_dn(sf))
            def _():
                out_ref[p, y, :, cols(c)] = jnp.where(
                    number >= plane_end, dn_recv[p, :, cols(c)], out_ref[p, y, :, cols(c)])

            @pl.when(gets_up(sf))
            def _():
                out_ref[p, y, :, cols(c)] = jnp.where(
                    number < plane_start, up_recv[p, :, cols(c)], out_ref[p, y, :, cols(c)])

            copy_f(sf, y).start()

    own = pltpu.make_async_copy(gb, gc.at[m], l_sem.at[2])
    own.start()
    own.wait()
    for d in range(1, parts):
        copy_c(d).wait()

    @pl.loop(0, total)
    def _(i):
        g = jnp.int32(0)
        for q in range(1, groups):
            g = g + (starts_ref[q] <= i).astype(jnp.int32)
        j = jnp.clip(i - starts_ref[g], 0, keep_most - 1)
        gout_ref[i] = gc[j // ks, g, lax.rem(j, ks)]

    @pl.loop(0, steps)
    def _(s):
        copy_f(s, y).wait_send()
        copy_f(s, 1 - y).wait_recv()

        @pl.when(gives_dn(s))
        def _():
            copy_dn(s).wait_send()

        @pl.when(gives_up(s))
        def _():
            copy_up(s).wait_send()


def exchange(count, hid, grad, groups, parts, total):
    keep_most, _, wide = hid.shape
    part = grad.shape[2]
    pairs = total // 2
    ks = keep_most // parts
    block = part * parts // groups
    bf16 = jnp.bfloat16
    chunks = 2 if wide % 256 == 0 else 1
    steps = chunks * pairs
    count = jnp.broadcast_to(count.reshape(1, 1), (1, 128))
    dma = pltpu.SemaphoreType.DMA
    chain = pltpu.VMEM((pairs, SEQ, wide), bf16)
    return pl.pallas_call(
        functools.partial(exchange_kernel, groups, parts, keep_most, total, chunks),
        out_shape=[
            jax.ShapeDtypeStruct((pairs, 2, SEQ, wide), bf16),
            jax.ShapeDtypeStruct((total, SEQ, block), bf16),
        ],
        in_specs=[
            pl.BlockSpec(memory_space=pltpu.VMEM),
            pl.BlockSpec(memory_space=pltpu.VMEM),
            pl.BlockSpec(memory_space=pltpu.VMEM),
        ],
        out_specs=[pl.BlockSpec(memory_space=pltpu.VMEM)] * 2,
        scratch_shapes=[
            pltpu.VMEM((groups, 1, 128), jnp.int32),
            pltpu.SMEM((groups, 1, 128), jnp.int32),
            pltpu.SMEM((groups + 1,), jnp.int32),
            pltpu.VMEM((keep_most // 2, SEQ, wide), bf16),
            [pltpu.VMEM((keep_most // 2, SEQ, wide // chunks), bf16)] * chunks,
            chain, chain, chain, chain, chain,
            pltpu.VMEM((parts, ks, SEQ, part), bf16),
            pltpu.VMEM((groups, ks, SEQ, block), bf16),
            pltpu.VMEM((parts, groups, ks, SEQ, block), bf16),
            dma((chunks * keep_most // 2,)), dma((chunks * keep_most // 2,)),
            dma((steps,)), dma((steps,)), dma((steps,)), dma((steps,)), dma((steps,)), dma((steps,)),
            dma((parts,)), dma((parts,)), dma((groups,)), dma((groups,)), dma((parts,)), dma((parts,)),
            dma((groups,)), dma((groups,)), dma((5,)),
        ],
        compiler_params=pltpu.CompilerParams(
            collective_id=0, has_side_effects=True, vmem_limit_bytes=60 * 1024 * 1024
        ),
    )(count, hid, grad)


def on_device(gate_act, up_act, upstream, kept_index, kept_count):
    groups, parts = lax.axis_size("batch"), lax.axis_size("mp")
    share = groups // 2
    total = groups * share
    wide, part = gate_act.shape[1], upstream.shape[1]
    hid, grad = pick(
        kept_index[0],
        gate_act.reshape(CAND, SEQ, wide),
        up_act.reshape(CAND, SEQ, wide),
        upstream.reshape(CAND, SEQ, part),
    )
    rows, columns = exchange(kept_count, hid, grad, groups, parts, total)
    summed = lax.dot_general(
        columns.reshape(total * SEQ, columns.shape[2]),
        rows.reshape(total * SEQ, wide),
        (((0,), (0,)), ((), ())),
        preferred_element_type=jnp.float32,
    )
    return (summed * (1.0 / math.sqrt(total * SEQ))).astype(jnp.bfloat16)


def solution(mesh):
    placed = (P("batch", "mp"), P("batch", "mp"), P("batch", "mp"), P("batch", None), P("batch"))
    return jax.shard_map(
        on_device, mesh=mesh, in_specs=placed, out_specs=P("batch", "mp"), check_vma=False
    )
```

time: 169 us -> 125 us (0.74)
  Pallas kernels: 146 us -> 113 us
  blocking collectives: 9.54 us -> 0 us
    pallas_call x1, Pallas kernels: 139 us -> 106 us  [exchange(): pl.pallas_call(functools.partial(exchange_kernel, groups, parts, keep_mos...]
    unnamed x1 -> x0, blocking collectives: 9.54 us -> none
    unnamed x3 -> x0, local copies, waits for them, and re-layouts: 2 us -> none
where the time goes in v2:
time: 125 us; the launch traced here: 124 us
  Pallas kernels  113 us (90%)
  matrix products  10.3 us (8%)
    pallas_call x1, Pallas kernels, exchange(): pl.pallas_call(functools.partial(exchange_kernel, groups, parts, keep_mos...  106 us
    dot_general x1, matrix products, on_device(): lax.dot_general(columns.reshape(total * SEQ, columns.shape[2]), rows.resh...  10.3 us
    pallas_call x1, Pallas kernels, pick(): pl.pallas_call(pick_kernel, grid_spec=pltpu.PrefetchScalarGridSpec(num_sc...  6.88 us

profile of v2, /device:TPU:1, one launch (start us, length us, event | category | flops | bytes accessed | tf_op | source)
XLA Modules:
  0.0 124.4 jit_solution(13226311418976749341)
XLA Ops:
  0.7 0.5 broadcast_in_dim.8.count_ref
  1.1 6.9 %shard_map.55 = (bf16[8,24,3584]{2,1,0:T(8,128)(2,1)}, bf16[8,24,2048]{2,1,0:T(8,128)(2,1)}) custom-call(s32[8]{0:T(128)} %bitcast.13, bf16[32,24,3584]{2,1,0:T(8,128)(2,1)} %bitcast.10, bf16[32,24,3584]{2,1,0:T(8,128)(2,1)} %bitcast.11, bf16[32,24,2048]{2,1,0:T(8,128)(2,1)} %bitcast.12), custom_call_target="tpu_custom_call" | custom-call | tf_op jit(solution)/shard_map/pallas_call | solution.py:33
  8.0 106.1 %shard_map.56 = (bf16[16,2,24,3584]{3,2,1,0:T(8,128)(2,1)}, bf16[32,24,1024]{2,1,0:T(8,128)(2,1)}) custom-call(s32[1,128]{1,0:T(1,128)} %broadcast_in_dim.8.count_ref, bf16[8,24,3584]{2,1,0:T(8,128)(2,1)} %get-tuple-element.9.hid_ref, bf16[8,24,2048]{2,1,0:T(8,128)(2,1)} %get-tuple-element.10.grad_ref), custom_call_target="tpu_custom_call" | custom-call | tf_op jit(solution)/shard_map/pallas_call | solution.py:331
  114.1 10.3 %multiply_convert_fusion = bf16[1024,3584]{1,0:T(8,128)(2,1)} fusion(bf16[768,1024]{1,0:T(8,128)(2,1)} %bitcast.15, bf16[768,3584]{1,0:T(8,128)(2,1)} %bitcast.14), kind=kOutput, calls=%fused_computation | convolution fusion | flops 5644484608 | bytes 14417920 | tf_op jit(solution)/shard_map/dot_general | solution.py:376

commit v3 on v2

--- a/solution.py
+++ b/solution.py
@@ -11,37 +11,48 @@
 SEQ = 24
 CAND = 32
 MESH = pl.DeviceIdType.MESH
-LEAD = 3
-
-
-def pick_kernel(index_ref, gate_ref, up_ref, up_grad_ref, hidden_ref, grad_ref):
-    gate = gate_ref[...].astype(jnp.float32)
-    hidden_ref[...] = (jax.nn.silu(gate) * up_ref[...].astype(jnp.float32)).astype(jnp.bfloat16)
-    grad_ref[...] = up_grad_ref[...]
+LEAD = 4
+
+
+def pick_kernel(keep_most, index_ref, gate_all, up_all, grad_all, hidden_ref, grad_ref, gate, up, sems):
+    def copies(j):
+        at = index_ref[j]
+        return (
+            pltpu.make_async_copy(gate_all.at[at], gate.at[j], sems.at[0, j]),
+            pltpu.make_async_copy(up_all.at[at], up.at[j], sems.at[1, j]),
+            pltpu.make_async_copy(grad_all.at[at], grad_ref.at[j], sems.at[2, j]),
+        )
+
+    for j in range(keep_most):
+        for copy in copies(j)[:2]:
+            copy.start()
+    for j in range(keep_most):
+        copies(j)[2].start()
+
+    @pl.loop(0, keep_most)
+    def _(j):
+        for copy in copies(j)[:2]:
+            copy.wait()
+        v = gate[j].astype(jnp.float32)
+        hidden_ref[j] = (jax.nn.silu(v) * up[j].astype(jnp.float32)).astype(jnp.bfloat16)
+
+    for j in range(keep_most):
+        copies(j)[2].wait()
 
 
 def pick(picked, gate_all, up_all, grad_all):
     keep_most = picked.shape[0]
-
-    def block(width):
-        return pl.BlockSpec((1, SEQ, width), lambda j, index: (index[j], 0, 0))
-
-    def out_block(width):
-        return pl.BlockSpec((1, SEQ, width), lambda j, index: (j, 0, 0))
-
     wide, part = gate_all.shape[2], grad_all.shape[2]
+    rows = pltpu.VMEM((keep_most, SEQ, wide), jnp.bfloat16)
     return pl.pallas_call(
-        pick_kernel,
-        grid_spec=pltpu.PrefetchScalarGridSpec(
-            num_scalar_prefetch=1,
-            grid=(keep_most,),
-            in_specs=[block(wide), block(wide), block(part)],
-            out_specs=[out_block(wide), out_block(part)],
-        ),
+        functools.partial(pick_kernel, keep_most),
+        in_specs=[pl.BlockSpec(memory_space=pltpu.SMEM)] + [pl.BlockSpec(memory_space=pl.ANY)] * 3,
+        out_specs=[pl.BlockSpec(memory_space=pltpu.VMEM)] * 2,
         out_shape=[
             jax.ShapeDtypeStruct((keep_most, SEQ, wide), jnp.bfloat16),
             jax.ShapeDtypeStruct((keep_most, SEQ, part), jnp.bfloat16),
         ],
+        scratch_shapes=[rows, rows, pltpu.SemaphoreType.DMA((3, keep_most))],
     )(picked, gate_all, up_all, grad_all)
 
 
@@ -225,7 +236,7 @@
             def _():
                 place(t, c)
 
-        @pl.when(t == steps // 3)
+        @pl.when(t == steps // 2)
         def _():
             for d in range(1, groups):
                 copy_b(d).wait()
@@ -323,7 +334,7 @@
     ks = keep_most // parts
     block = part * parts // groups
     bf16 = jnp.bfloat16
-    chunks = 2 if wide % 256 == 0 else 1
+    chunks = 4 if wide % 512 == 0 else 1
     steps = chunks * pairs
     count = jnp.broadcast_to(count.reshape(1, 1), (1, 128))
     dma = pltpu.SemaphoreType.DMA

time: 125 us -> 121 us (0.968)
  Pallas kernels: 113 us -> 110 us
    pallas_call x1, Pallas kernels: 6.88 us -> 4.27 us  [pick(): pl.pallas_call(functools.partial(pick_kernel, keep_most), in_specs=[pl.Bl...]
where the time goes in v3:
time: 121 us
  Pallas kernels  110 us (91%)
  matrix products  10.3 us (9%)
    pallas_call x1, Pallas kernels, exchange(): pl.pallas_call(functools.partial(exchange_kernel, groups, parts, keep_mos...  105 us
    dot_general x1, matrix products, on_device(): lax.dot_general(columns.reshape(total * SEQ, columns.shape[2]), rows.resh...  10.3 us
    pallas_call x1, Pallas kernels, pick(): pl.pallas_call(functools.partial(pick_kernel, keep_most), in_specs=[pl.Bl...  4.27 us

profile of v3, /device:TPU:1, one launch (start us, length us, event | category | flops | bytes accessed | tf_op | source)
XLA Modules:
  0.0 121.0 jit_solution(12887612322114168745)
XLA Ops:
  0.7 0.5 broadcast_in_dim.8.count_ref
  1.1 4.3 %shard_map.55 = (bf16[8,24,3584]{2,1,0:T(8,128)(2,1)}, bf16[8,24,2048]{2,1,0:T(8,128)(2,1)}) custom-call(s32[8]{0:T(128)} %bitcast.13, bf16[32,24,3584]{2,1,0:T(8,128)(2,1)} %bitcast.10, bf16[32,24,3584]{2,1,0:T(8,128)(2,1)} %bitcast.11, bf16[32,24,2048]{2,1,0:T(8,128)(2,1)} %bitcast.12), custom_call_target="tpu_custom_call" | custom-call | tf_op jit(solution)/shard_map/pallas_call | solution.py:47
  5.4 105.3 %shard_map.56 = (bf16[16,2,24,3584]{3,2,1,0:T(8,128)(2,1)}, bf16[32,24,1024]{2,1,0:T(8,128)(2,1)}) custom-call(s32[1,128]{1,0:T(1,128)} %broadcast_in_dim.8.count_ref, bf16[8,24,3584]{2,1,0:T(8,128)(2,1)} %get-tuple-element.9.hid_ref, bf16[8,24,2048]{2,1,0:T(8,128)(2,1)} %get-tuple-element.10.grad_ref), custom_call_target="tpu_custom_call" | custom-call | tf_op jit(solution)/shard_map/pallas_call | solution.py:342
  110.7 10.3 %multiply_convert_fusion = bf16[1024,3584]{1,0:T(8,128)(2,1)} fusion(bf16[768,1024]{1,0:T(8,128)(2,1)} %bitcast.15, bf16[768,3584]{1,0:T(8,128)(2,1)} %bitcast.14), kind=kOutput, calls=%fused_computation | convolution fusion | flops 5644484608 | bytes 14417920 | tf_op jit(solution)/shard_map/dot_general | solution.py:387

commit v4 on v3

--- a/solution.py
+++ b/solution.py
@@ -60,9 +60,9 @@
     groups, parts, keep_most, total, chunks,
     count_ref, hid_ref, grad_ref, out_ref, gout_ref,
     counts_in, counts_ref, starts_ref,
-    y_send, y_recv, loc, dn_recv, dn_send, up_recv, up_send, ga, gb, gc,
+    y_send, y_recv, fin, loc, dn_recv, dn_send, up_recv, up_send, ga, gb, gc,
     ys_sem, yr_sem, dns_sem, dnr_sem, ups_sem, upr_sem, fs_sem, fr_sem,
-    as_sem, ar_sem, bs_sem, br_sem, cs_sem, cr_sem, ns_sem, nr_sem, l_sem,
+    as_sem, ar_sem, bs_sem, br_sem, cs_sem, cr_sem, ns_sem, nr_sem, o_sem, l_sem,
 ):
     b, m = lax.axis_index("batch"), lax.axis_index("mp")
     planes, pairs = groups // 2, total // 2
@@ -144,9 +144,13 @@
     def copy_f(s, side):
         p, c = lax.rem(s, pairs), s // pairs
         return pltpu.make_async_remote_copy(
-            src_ref=out_ref.at[p, side, :, cols(c)], dst_ref=out_ref.at[p, side, :, cols(c)],
+            src_ref=fin.at[p, :, cols(c)], dst_ref=out_ref.at[p, side, :, cols(c)],
             send_sem=fs_sem.at[s], recv_sem=fr_sem.at[s],
             device_id=(peer, m), device_id_type=MESH)
+
+    def copy_o(s):
+        p, c = lax.rem(s, pairs), s // pairs
+        return pltpu.make_async_copy(fin.at[p, :, cols(c)], out_ref.at[p, y, :, cols(c)], o_sem.at[s])
 
     for d in range(1, groups):
         copy_n(d).start()
@@ -285,19 +289,20 @@
         def _():
             p, c = lax.rem(sf, pairs), sf // pairs
             number = 2 * p + y
-            out_ref[p, y, :, cols(c)] = loc[p, :, cols(c)]
+            fin[p, :, cols(c)] = loc[p, :, cols(c)]
 
             @pl.when(gets_dn(sf))
             def _():
-                out_ref[p, y, :, cols(c)] = jnp.where(
-                    number >= plane_end, dn_recv[p, :, cols(c)], out_ref[p, y, :, cols(c)])
+                fin[p, :, cols(c)] = jnp.where(
+                    number >= plane_end, dn_recv[p, :, cols(c)], fin[p, :, cols(c)])
 
             @pl.when(gets_up(sf))
             def _():
-                out_ref[p, y, :, cols(c)] = jnp.where(
-                    number < plane_start, up_recv[p, :, cols(c)], out_ref[p, y, :, cols(c)])
+                fin[p, :, cols(c)] = jnp.where(
+                    number < plane_start, up_recv[p, :, cols(c)], fin[p, :, cols(c)])
 
             copy_f(sf, y).start()
+            copy_o(sf).start()
 
     own = pltpu.make_async_copy(gb, gc.at[m], l_sem.at[2])
     own.start()
@@ -316,6 +321,7 @@
     @pl.loop(0, steps)
     def _(s):
         copy_f(s, y).wait_send()
+        copy_o(s).wait()
         copy_f(s, 1 - y).wait_recv()
 
         @pl.when(gives_dn(s))
@@ -350,21 +356,21 @@
             pl.BlockSpec(memory_space=pltpu.VMEM),
             pl.BlockSpec(memory_space=pltpu.VMEM),
         ],
-        out_specs=[pl.BlockSpec(memory_space=pltpu.VMEM)] * 2,
+        out_specs=[pl.BlockSpec(memory_space=pl.ANY), pl.BlockSpec(memory_space=pltpu.VMEM)],
         scratch_shapes=[
             pltpu.VMEM((groups, 1, 128), jnp.int32),
             pltpu.SMEM((groups, 1, 128), jnp.int32),
             pltpu.SMEM((groups + 1,), jnp.int32),
             pltpu.VMEM((keep_most // 2, SEQ, wide), bf16),
             [pltpu.VMEM((keep_most // 2, SEQ, wide // chunks), bf16)] * chunks,
-            chain, chain, chain, chain, chain,
+            chain, chain, chain, chain, chain, chain,
             pltpu.VMEM((parts, ks, SEQ, part), bf16),
             pltpu.VMEM((groups, ks, SEQ, block), bf16),
             pltpu.VMEM((parts, groups, ks, SEQ, block), bf16),
             dma((chunks * keep_most // 2,)), dma((chunks * keep_most // 2,)),
             dma((steps,)), dma((steps,)), dma((steps,)), dma((steps,)), dma((steps,)), dma((steps,)),
             dma((parts,)), dma((parts,)), dma((groups,)), dma((groups,)), dma((parts,)), dma((parts,)),
-            dma((groups,)), dma((groups,)), dma((5,)),
+            dma((groups,)), dma((groups,)), dma((steps,)), dma((5,)),
         ],
         compiler_params=pltpu.CompilerParams(
             collective_id=0, has_side_effects=True, vmem_limit_bytes=60 * 1024 * 1024

time: 121 us -> 120 us (level)
  no operation moved by 1% of the time
where the time goes in v4:
time: 120 us
  Pallas kernels  109 us (91%)
  matrix products  10.3 us (9%)
    pallas_call x1, Pallas kernels, exchange(): pl.pallas_call(functools.partial(exchange_kernel, groups, parts, keep_mos...  104 us
    dot_general x1, matrix products, on_device(): lax.dot_general(columns.reshape(total * SEQ, columns.shape[2]), rows.resh...  10.3 us
    pallas_call x1, Pallas kernels, pick(): pl.pallas_call(functools.partial(pick_kernel, keep_most), in_specs=[pl.Bl...  4.27 us

profile of v4, /device:TPU:1, one launch (start us, length us, event | category | flops | bytes accessed | tf_op | source)
XLA Modules:
  0.0 119.9 jit_solution(16963997181030794122)
XLA Ops:
  0.7 0.5 broadcast_in_dim.8.count_ref
  1.1 4.3 %shard_map.55 = (bf16[8,24,3584]{2,1,0:T(8,128)(2,1)}, bf16[8,24,2048]{2,1,0:T(8,128)(2,1)}) custom-call(s32[8]{0:T(128)} %bitcast.13, bf16[32,24,3584]{2,1,0:T(8,128)(2,1)} %bitcast.10, bf16[32,24,3584]{2,1,0:T(8,128)(2,1)} %bitcast.11, bf16[32,24,2048]{2,1,0:T(8,128)(2,1)} %bitcast.12), custom_call_target="tpu_custom_call" | custom-call | tf_op jit(solution)/shard_map/pallas_call | solution.py:47
  5.4 104.2 %shard_map.56 = (bf16[16,2,24,3584]{3,2,1,0:T(8,128)(2,1)}, bf16[32,24,1024]{2,1,0:T(8,128)(2,1)}) custom-call(s32[1,128]{1,0:T(1,128)} %broadcast_in_dim.8.count_ref, bf16[8,24,3584]{2,1,0:T(8,128)(2,1)} %get-tuple-element.9.hid_ref, bf16[8,24,2048]{2,1,0:T(8,128)(2,1)} %get-tuple-element.10.grad_ref), custom_call_target="tpu_custom_call" | custom-call | tf_op jit(solution)/shard_map/pallas_call | solution.py:348
  109.7 10.3 %multiply_convert_fusion = bf16[1024,3584]{1,0:T(8,128)(2,1)} fusion(bf16[768,1024]{1,0:T(8,128)(2,1)} %bitcast.15, bf16[768,3584]{1,0:T(8,128)(2,1)} %bitcast.14), kind=kOutput, calls=%fused_computation | convolution fusion | flops 5644484608 | bytes 14417920 | tf_op jit(solution)/shard_map/dot_general | solution.py:393

commit v5 on v4

--- a/solution.py
+++ b/solution.py
@@ -11,7 +11,7 @@
 SEQ = 24
 CAND = 32
 MESH = pl.DeviceIdType.MESH
-LEAD = 4
+LEAD = 6
 
 
 def pick_kernel(keep_most, index_ref, gate_all, up_all, grad_all, hidden_ref, grad_ref, gate, up, sems):
@@ -240,7 +240,7 @@
             def _():
                 place(t, c)
 
-        @pl.when(t == steps // 2)
+        @pl.when(t == steps // 3)
         def _():
             for d in range(1, groups):
                 copy_b(d).wait()

time: 120 us -> 122 us (1.017)
    pallas_call x1, Pallas kernels: 104 us -> 106 us  [exchange(): pl.pallas_call(functools.partial(exchange_kernel, groups, parts, keep_mos...]
where the time goes in v5:
time: 122 us
  Pallas kernels  110 us (90%)
  matrix products  10.3 us (8%)
    pallas_call x1, Pallas kernels, exchange(): pl.pallas_call(functools.partial(exchange_kernel, groups, parts, keep_mos...  106 us
    dot_general x1, matrix products, on_device(): lax.dot_general(columns.reshape(total * SEQ, columns.shape[2]), rows.resh...  10.3 us
    pallas_call x1, Pallas kernels, pick(): pl.pallas_call(functools.partial(pick_kernel, keep_most), in_specs=[pl.Bl...  4.27 us

profile of v5, /device:TPU:1, one launch (start us, length us, event | category | flops | bytes accessed | tf_op | source)
XLA Modules:
  0.0 121.5 jit_solution(6014830551438188345)
XLA Ops:
  0.7 0.5 broadcast_in_dim.8.count_ref
  1.1 4.3 %shard_map.55 = (bf16[8,24,3584]{2,1,0:T(8,128)(2,1)}, bf16[8,24,2048]{2,1,0:T(8,128)(2,1)}) custom-call(s32[8]{0:T(128)} %bitcast.13, bf16[32,24,3584]{2,1,0:T(8,128)(2,1)} %bitcast.10, bf16[32,24,3584]{2,1,0:T(8,128)(2,1)} %bitcast.11, bf16[32,24,2048]{2,1,0:T(8,128)(2,1)} %bitcast.12), custom_call_target="tpu_custom_call" | custom-call | tf_op jit(solution)/shard_map/pallas_call | solution.py:47
  5.4 105.8 %shard_map.56 = (bf16[16,2,24,3584]{3,2,1,0:T(8,128)(2,1)}, bf16[32,24,1024]{2,1,0:T(8,128)(2,1)}) custom-call(s32[1,128]{1,0:T(1,128)} %broadcast_in_dim.8.count_ref, bf16[8,24,3584]{2,1,0:T(8,128)(2,1)} %get-tuple-element.9.hid_ref, bf16[8,24,2048]{2,1,0:T(8,128)(2,1)} %get-tuple-element.10.grad_ref), custom_call_target="tpu_custom_call" | custom-call | tf_op jit(solution)/shard_map/pallas_call | solution.py:348
  111.3 10.3 %multiply_convert_fusion = bf16[1024,3584]{1,0:T(8,128)(2,1)} fusion(bf16[768,1024]{1,0:T(8,128)(2,1)} %bitcast.15, bf16[768,3584]{1,0:T(8,128)(2,1)} %bitcast.14), kind=kOutput, calls=%fused_computation | convolution fusion | flops 5644484608 | bytes 14417920 | tf_op jit(solution)/shard_map/dot_general | solution.py:393
